TPU v7x, 256 devices: a whole 4x4x8 slice. The times are simulated.
256 devices in a mesh: seq: 32 (over y, x, core), rep: 8 (over z).
Axes of the slice: x: 4, y: 4, z: 8, core: 2. Of those that a mesh axis runs over, the one named last changes fastest.
Arguments:
- tokens: bfloat16 [8, 4096, 1024], P('rep', 'seq'), may hold values from -16 to 16
- cotangent: bfloat16 [8, 4096, 1024], P('rep', 'seq'), may hold values from -6 to 6
- weights: bfloat16 [4, 1024, 512], replicated, may hold values from -0.1875 to 0.1875
- neighbour_lists: int32 [8, 32, 27], P('rep'), may hold values from 0 to 31, as said below
- neighbour_counts: int32 [8, 32], P('rep'), may hold values from 1 to 27, as said below
Outputs:
- output: bfloat16 [8, 4096, 1024], P('rep', 'seq')
- d_inputs: bfloat16 [8, 4096, 1024], P('rep', 'seq')
- weight_grads: float32 [4, 1024, 512], P(None, ('seq', 'rep'))
Inputs may be any that keep to these rules, and one draw needn't show every extreme that they name: `neighbour_lists`: slot 0 of every list is the block itself; the live slots of a list name distinct blocks of the same replica's slab; dead slots hold the block's own position. `neighbour_counts`: in each replica some block has min(27, 32) live slots.
All inputs are finite; a program needn't handle non-finite values.
Results may differ from a plain program's by a relative error of at most 0.023.
The roundings to bfloat16 on the way count: a program that leaves them out, or rounds other values in their place, can miss the bound.
Values may be sent and summed in bfloat16 or wider, within the bound.
No kernel may reach another device: no remote copies, remote signals or barrier semaphores. Data moves between devices by JAX's collectives and lax.ppermute only.
A program may use at most 128 MiB of HBM per device.

v0:
```python
import math
import jax
import jax.numpy as jnp
from jax import lax
from jax.sharding import PartitionSpec as P

HEADS = 8
HEAD_DIM = 64
BLOCK = 128
MAXN = 27


def split_heads(matrix):
    return matrix.reshape(matrix.shape[:-1] + (HEADS, HEAD_DIM))


def body(tokens, cotangent, weights, neighbour_lists, neighbour_counts):
    score_scale = 1.0 / math.sqrt(HEAD_DIM)
    inputs = tokens[0]
    upstream = cotangent[0]
    row_count = inputs.shape[0]
    local_blocks = row_count // BLOCK
    w_query, w_key, w_value, w_out = (weights[0], weights[1], weights[2], weights[3])
    queries = (
        jnp.dot(inputs, w_query, preferred_element_type=jnp.float32)
        .astype(jnp.bfloat16)
        .reshape(local_blocks, BLOCK, -1)
    )
    key_rows = (
        jnp.dot(inputs, w_key, preferred_element_type=jnp.float32)
        .astype(jnp.bfloat16)
        .reshape(local_blocks, BLOCK, -1)
    )
    value_rows = (
        jnp.dot(inputs, w_value, preferred_element_type=jnp.float32)
        .astype(jnp.bfloat16)
        .reshape(local_blocks, BLOCK, -1)
    )
    all_keys, all_values = (
        lax.all_gather(key_rows, "seq", axis=0, tiled=True),
        lax.all_gather(value_rows, "seq", axis=0, tiled=True),
    )
    slab_blocks = all_keys.shape[0]
    first_block = lax.axis_index("seq") * local_blocks
    lists_all = neighbour_lists[0]
    counts_all = neighbour_counts[0]
    my_lists = lax.dynamic_slice_in_dim(lists_all, first_block, local_blocks, 0)
    my_counts = lax.dynamic_slice_in_dim(counts_all, first_block, local_blocks, 0)
    slot_keys = split_heads(
        jnp.take(all_keys, my_lists, axis=0).reshape(local_blocks, MAXN * BLOCK, -1)
    )
    slot_values = split_heads(
        jnp.take(all_values, my_lists, axis=0).reshape(local_blocks, MAXN * BLOCK, -1)
    )
    query_heads = split_heads(queries)
    scores = (
        jnp.einsum("bqhd,bkhd->bhqk", query_heads, slot_keys, preferred_element_type=jnp.float32)
        * score_scale
    )
    live_cols = (jnp.arange(MAXN * BLOCK) // BLOCK)[None, :] < my_counts[:, None]
    scores = jnp.where(live_cols[:, None, None, :], scores, -1e30)
    row_max = jnp.max(scores, axis=-1)
    exponent = jnp.exp(scores - row_max[..., None])
    totals = jnp.sum(exponent, axis=-1)
    mixed = jnp.einsum(
        "bhqk,bkhd->bqhd",
        exponent.astype(jnp.bfloat16),
        slot_values,
        preferred_element_type=jnp.float32,
    )
    attended = (
        (mixed / jnp.transpose(totals, (0, 2, 1))[..., None])
        .astype(jnp.bfloat16)
        .reshape(row_count, -1)
    )
    output = lax.dot_general(
        attended, w_out, (((1,), (1,)), ((), ())), preferred_element_type=jnp.float32
    ).astype(jnp.bfloat16)
    d_attended = jnp.dot(upstream, w_out, preferred_element_type=jnp.float32).astype(jnp.bfloat16)
    grad_out = lax.dot_general(
        upstream, attended, (((0,), (0,)), ((), ())), preferred_element_type=jnp.float32
    )
    d_blocks = d_attended.reshape(local_blocks, BLOCK, -1)
    d_heads = split_heads(d_blocks)
    attended_heads = split_heads(attended.reshape(local_blocks, BLOCK, -1))
    row_delta = jnp.transpose(
        jnp.sum(d_heads.astype(jnp.float32) * attended_heads.astype(jnp.float32), axis=-1),
        (0, 2, 1),
    )
    normed = exponent / totals[..., None]
    d_probs = jnp.einsum(
        "bqhd,bkhd->bhqk", d_heads, slot_values, preferred_element_type=jnp.float32
    )
    d_scores = (normed * (d_probs - row_delta[..., None])).astype(jnp.bfloat16)
    d_queries = (
        (
            jnp.einsum("bhqk,bkhd->bqhd", d_scores, slot_keys, preferred_element_type=jnp.float32)
            * score_scale
        )
        .astype(jnp.bfloat16)
        .reshape(row_count, -1)
    )
    gathered_query, gathered_dattn = (
        lax.all_gather(queries, "seq", axis=0, tiled=True),
        lax.all_gather(d_blocks, "seq", axis=0, tiled=True),
    )
    gathered_max, gathered_total, gathered_delta = (
        lax.all_gather(row_max, "seq", axis=0, tiled=True),
        lax.all_gather(totals, "seq", axis=0, tiled=True),
        lax.all_gather(row_delta, "seq", axis=0, tiled=True),
    )
    owners = first_block + jnp.arange(local_blocks)
    live_slots = jnp.arange(MAXN)[None, :] < counts_all[:, None]
    listed = jnp.any(
        (lists_all[:, :, None] == owners[None, None, :]) & live_slots[:, :, None], axis=1
    )
    groups = slab_blocks // 8
    own_keys = split_heads(key_rows)
    own_values = split_heads(value_rows)

    def regroup(matrix):
        return matrix.reshape((groups, 8) + matrix.shape[1:])

    def accumulate(carry, group_data):
        group_query, group_dattn, group_max, group_total, group_delta, group_listed = group_data
        group_query = split_heads(group_query)
        group_dattn = split_heads(group_dattn)
        group_scores = (
            jnp.einsum(
                "cqhd,ikhd->cihqk", group_query, own_keys, preferred_element_type=jnp.float32
            )
            * score_scale
        )
        group_scores = jnp.where(group_listed[:, :, None, None, None], group_scores, -1e30)
        group_probs = (
            jnp.exp(group_scores - group_max[:, None, :, :, None])
            / group_total[:, None, :, :, None]
        )
        group_dprobs = jnp.einsum(
            "cqhd,ikhd->cihqk", group_dattn, own_values, preferred_element_type=jnp.float32
        )
        group_dscores = (group_probs * (group_dprobs - group_delta[:, None, :, :, None])).astype(
            jnp.bfloat16
        )
        key_next = carry[0] + jnp.einsum(
            "cihqk,cqhd->ikhd", group_dscores, group_query, preferred_element_type=jnp.float32
        )
        value_next = carry[1] + jnp.einsum(
            "cihqk,cqhd->ikhd",
            group_probs.astype(jnp.bfloat16),
            group_dattn,
            preferred_element_type=jnp.float32,
        )
        return ((key_next, value_next), None)

    zero_sum = jnp.zeros((local_blocks, BLOCK, HEADS, HEAD_DIM), jnp.float32)
    group_inputs = (
        regroup(gathered_query),
        regroup(gathered_dattn),
        regroup(gathered_max),
        regroup(gathered_total),
        regroup(gathered_delta),
        regroup(listed),
    )
    (key_heads, value_heads), _ = lax.scan(accumulate, (zero_sum, zero_sum), group_inputs)
    key_sum = (key_heads * score_scale).reshape(local_blocks, BLOCK, -1)
    value_sum = value_heads.reshape(local_blocks, BLOCK, -1)
    d_keys = key_sum.astype(jnp.bfloat16).reshape(row_count, -1)
    d_values = value_sum.astype(jnp.bfloat16).reshape(row_count, -1)
    stacked = jnp.concatenate([d_queries, d_keys, d_values], axis=1)
    w_joined = jnp.concatenate([w_query, w_key, w_value], axis=1)
    d_inputs = lax.dot_general(
        stacked, w_joined, (((1,), (1,)), ((), ())), preferred_element_type=jnp.float32
    ).astype(jnp.bfloat16)
    grad_joined = lax.dot_general(
        inputs, stacked, (((0,), (0,)), ((), ())), preferred_element_type=jnp.float32
    )
    width_model = inputs.shape[1]
    grad_three = jnp.transpose(grad_joined.reshape(width_model, 3, -1), (1, 0, 2))
    grads = jnp.concatenate([grad_three, grad_out[None]], axis=0)
    summed = lax.psum_scatter(grads, ("seq", "rep"), scatter_dimension=1, tiled=True)
    return (output[None], d_inputs[None], summed)


def solution(mesh):
    placed = (
        P("rep", "seq", None),
        P("rep", "seq", None),
        P(),
        P("rep", None, None),
        P("rep", None),
    )
    return jax.shard_map(
        body,
        mesh=mesh,
        in_specs=placed,
        out_specs=(P("rep", "seq", None), P("rep", "seq", None), P(None, ("seq", "rep"), None)),
        check_vma=False,
    )
```

profile of v0, /device:TPU:97, one launch (start us, length us, event | category | flops | bytes accessed | tf_op | source)
XLA Modules:
  0.0 669.6 jit_solution(1449751588284421774)
XLA Ops:
  8.1 2.2 convolution_convert_fusion.4
  10.4 2.2 convolution_convert_fusion.2
  12.6 2.3 convolution_convert_fusion.1
  15.0 2.2 convolution_convert_fusion.3
  24.6 39.4 %all-gather.11.cloned.1.call-done = bf16[4096,512]{1,0:T(8,128)(2,1)} async-done(((bf16[128,512]{1,0:T(8,128)(2,1)}), bf16[4096,512]{1,0:T(8,128)(2,1)}) %all-gather.11.cloned.1.call-update) | async-done | bytes 4194320 | tf_op jit(solution)/shard_map/all_gather | solution.py:41
  63.9 4.8 gather_fusion
  68.8 48.2 %all-gather.13.cloned.1.call-done = bf16[4096,512]{1,0:T(8,128)(2,1)} async-done(((bf16[128,512]{1,0:T(8,128)(2,1)}), bf16[4096,512]{1,0:T(8,128)(2,1)}) %all-gather.13.cloned.1.call-update) | async-done | bytes 4194320 | tf_op jit(solution)/shard_map/all_gather | solution.py:40
  117.0 4.8 gather_fusion.1
  121.8 6.7 bitcast_select_fusion.1
  128.4 7.8 %copy.59 = bf16[1,27,128,512]{2,1,3,0:T(8,128)(2,1)} copy(bf16[1,27,128,512]{3,2,1,0:T(8,128)(2,1)} %get-tuple-element.173) | data formatting | bytes 7077888 | tf_op jit(solution)/shard_map/jit(_take)/select_n | solution.py:50
  136.3 7.0 %reshape.273 = bf16[3456,8,64]{0,2,1:T(8,128)(2,1)} reshape(bf16[1,27,128,512]{2,1,3,0:T(8,128)(2,1)} %copy.59) | data formatting | bytes 7077888 | tf_op jit(solution)/shard_map/reshape.48
  143.2 7.8 %copy.57 = bf16[1,27,128,512]{2,1,3,0:T(8,128)(2,1)} copy(bf16[1,27,128,512]{3,2,1,0:T(8,128)(2,1)} %get-tuple-element.174) | data formatting | bytes 7077888 | tf_op jit(solution)/shard_map/jit(_take)/select_n | solution.py:53
  151.0 7.0 %reshape.270 = bf16[3456,8,64]{0,2,1:T(8,128)(2,1)} reshape(bf16[1,27,128,512]{2,1,3,0:T(8,128)(2,1)} %copy.57) | data formatting | bytes 7077888 | tf_op jit(solution)/shard_map/reshape.51
  158.0 9.3 %fusion.27 = (f32[8,128]{1,0:T(8,128)S(1)}, f32[8,128,3456]{2,1,0:T(8,128)}) fusion(pred[3456]{0:T(1024)(128)(4,1)S(1)} %fusion.69, bf16[128,8,64]{0,2,1:T(8,128)(2,1)S(1)} %bitcast.237, bf16[3456,8,64]{0,2,1:T(8,128)(2,1)} %reshape.273), kind=kOutput, calls=%fused_computation.36 | convolution fusion | flops 463600640 | bytes 17833344 | tf_op jit(solution)/shard_map/bqhd,bkhd->bhqk/dot_general | solution.py:57
  167.2 26.0 %all-gather.3 = f32[256,128]{1,0:T(8,128)} all-gather(f32[8,128]{1,0:T(8,128)S(1)} %get-tuple-element.175), channel_id=5, replica_groups=mesh['seq'=32,'rep'=8] {'seq'}, dimensions={0}, use_global_device_ids=true | all-gather | bytes 135168 | tf_op jit(solution)/shard_map/all_gather | solution.py:108
  193.2 8.2 %fusion.28 = f32[8,128]{1,0:T(8,128)S(1)} fusion(f32[8,128,3456]{2,1,0:T(8,128)} %get-tuple-element.176, f32[8,128]{1,0:T(8,128)S(1)} %get-tuple-element.175, pred[3456]{0:T(1024)(128)(4,1)S(1)} %fusion.69), kind=kLoop, calls=%fused_computation.38 | loop fusion | flops 14154752 | bytes 14167424 | tf_op jit(solution)/shard_map/reduce_sum | solution.py:64
  201.4 25.0 %all-gather.4 = f32[256,128]{1,0:T(8,128)} all-gather(f32[8,128]{1,0:T(8,128)S(1)} %fusion.28), channel_id=6, replica_groups=mesh['seq'=32,'rep'=8] {'seq'}, dimensions={0}, use_global_device_ids=true | all-gather | bytes 135168 | tf_op jit(solution)/shard_map/all_gather | solution.py:109
  226.4 9.1 %multiply_reduce_fusion = (f32[128,8]{0,1:T(8,128)S(1)}, bf16[1,128,8,64]{1,3,2,0:T(8,128)(2,1)}) fusion(f32[1,128,8,64]{1,3,2,0:T(8,128)S(1)} %bitcast.247, f32[128,8]{0,1:T(8,128)S(1)} %bitcast.254, bf16[3456,8,64]{0,2,1:T(8,128)(2,1)S(1)} %copy-done.3, f32[8,128,3456]{2,1,0:T(8,128)} %get-tuple-element.176, f32[8,128]{1,0:T(8,128)S(1)} %get-tuple-element.175, ...), kind=kOutput, calls=%fused_computation.81 | convolution fusion | flops 467467264 | bytes 18103680 | tf_op jit(solution)/shard_map/bhqk,bkhd->bqhd/dot_general | solution.py:65
  235.5 25.4 %all_gather.27 = f32[32,8,128]{2,1,0:T(8,128)} all-gather(f32[1,8,128]{2,1,0:T(8,128)S(1)} %bitcast.255), channel_id=1, replica_groups=mesh['seq'=32,'rep'=8] {'seq'}, dimensions={0}, use_global_device_ids=true | all-gather | bytes 135168 | tf_op jit(solution)/shard_map/all_gather | solution.py:110
  260.9 88.9 %while.13 = (s32[]{:T(128)}, f32[1,128,8,64]{1,3,2,0:T(8,128)}, f32[1,128,8,64]{1,3,2,0:T(8,128)}, bf16[4,8,128,512]{3,2,1,0:T(8,128)(2,1)}, pred[4,8,1]{1,2,0:T...) while((s32[]{:T(128)}, f32[1,128,8,64]{1,3,2,0:T(8,128)}, ...), condition=%wide.region_5.7_spmd.clone, body=%wide.region_4.6_spmd.clone.sunk | while | flops 545521664 | bytes 35356956 | solution.py:165
  260.9 1.7 constant_dynamic-slice_fusion.10
  266.2 5.4 fusion.112
  273.1 4.4 fusion.113
  277.5 2.2 fusion.114
  279.7 2.8 fusion.115
  283.2 1.7 constant_dynamic-slice_fusion.10
  288.4 5.4 fusion.112
  295.3 4.4 fusion.113
  299.7 2.2 fusion.114
  301.9 2.8 fusion.115
  305.4 1.7 constant_dynamic-slice_fusion.10
  310.6 5.4 fusion.112
  317.4 4.4 fusion.113
  321.9 2.2 fusion.114
  324.1 2.8 fusion.115
  332.8 5.4 fusion.112
  339.7 4.4 fusion.113
  344.1 2.2 fusion.114
  346.3 2.8 fusion.115
  351.7 10.6 %fusion.51 = bf16[8,64,128]{2,1,0:T(8,128)(2,1)S(1)} fusion(bf16[3456,8,64]{0,2,1:T(8,128)(2,1)} %reshape.273, bf16[128,8,64]{0,2,1:T(8,128)(2,1)} %bitcast.252, bf16[3456,8,64]{0,2,1:T(8,128)(2,1)} %reshape.270, f32[8,128,3456]{2,1,0:T(8,128)} %get-tuple-element.176, f32[8,128]{1,0:T(8,128)S(1)} %bitcast.256, f32[8,128]{1,0:T(8,128)S(1)} %fusion.28, ...), kind=kOutput, calls=%fused_computation.62 | convolution fusion | flops 930873344 | bytes 21511552 | tf_op jit(solution)/shard_map/bhqk,bkhd->bqhd/dot_general | solution.py:97
  362.3 3.6 fusion.64
  365.9 6.6 copy.70
  372.9 1.8 copy.71
  374.8 7.6 %pad_maximum_fusion = f32[4,1024,512]{2,1,0:T(8,128)} fusion(f32[1,1024,512]{2,1,0:T(8,128)} %copy.71, f32[3,1024,512]{2,1,0:T(8,128)} %bitcast.230), kind=kLoop, calls=%fused_computation.37 | loop fusion | flops 2097152 | bytes 16777216 | tf_op jit(solution)/shard_map/concatenate | solution.py:180
  382.4 2.1 slice_bitcast_fusion.1
  384.5 2.4 fusion.43
  386.9 1.9 fusion.44
  388.8 272.8 %all-reduce.3.cloned.1.call-done = f32[4,1024,512]{2,1,0:T(8,128)} async-done(((f32[4,1024,512]{2,1,0:T(8,128)}), f32[4,1024,512]{2,1,0:T(8,128)}) %all-reduce.3.cloned.1.call-update) | async-done | bytes 8388624
  (113 shorter events, 36.5 us)
Async XLA Ops:
  7.2 1.0 copy-start
  7.2 14.7 %copy-start.11 = (s32[1,32]{1,0:T(1,128)S(1)}, s32[1,32]{1,0:T(1,128)}, u32[]{:S(2)}) copy-start(s32[1,32]{1,0:T(1,128)} %param.13) | copy-start | bytes 388
  7.2 15.3 %copy-start.10 = (s32[1,32,27]{1,0,2:T(1,128)S(1)}, s32[1,32,27]{1,0,2:T(1,128)}, u32[]{:S(2)}) copy-start(s32[1,32,27]{1,0,2:T(1,128)} %param.12) | copy-start | bytes 10372
  7.2 56.7 %all-gather.11.cloned.1.call-start = ((), (), s32[]{:S(2)}) async-start(), calls=%async_computation | async-start | bytes 4325376 | tf_op jit(solution)/shard_map/all_gather | solution.py:41
  10.3 11.4 %copy-start.4 = (bf16[128,512]{1,0:T(8,128)(2,1)S(1)}, bf16[128,512]{1,0:T(8,128)(2,1)}, u32[]{:S(2)}) copy-start(bf16[128,512]{1,0:T(8,128)(2,1)} %convolution_convert_fusion.4) | copy-start | bytes 393220
  10.3 106.7 %all-gather.13.cloned.1.call-start = ((), (), s32[]{:S(2)}) async-start(), calls=%async_computation.1 | async-start | bytes 4325376 | tf_op jit(solution)/shard_map/all_gather | solution.py:40
  12.6 8.4 %copy-start.5 = (bf16[128,512]{1,0:T(8,128)(2,1)S(1)}, bf16[128,512]{1,0:T(8,128)(2,1)}, u32[]{:S(2)}) copy-start(bf16[128,512]{1,0:T(8,128)(2,1)} %convolution_convert_fusion.2) | copy-start | bytes 393220
  12.6 248.3 %all-gather.17.cloned.1.call-start = ((), (), s32[]{:S(2)}) async-start(), calls=%async_computation.3 | async-start | bytes 4325376 | tf_op jit(solution)/shard_map/all_gather | solution.py:105
  15.0 245.9 %all-gather.15.cloned.1.call-start = ((), (), s32[]{:S(2)}) async-start(), calls=%async_computation.2 | async-start | bytes 4325376 | tf_op jit(solution)/shard_map/all_gather | solution.py:104
  17.2 644.4 %all-reduce.3.cloned.1.call-start = ((), (), s32[]{:S(2)}) async-start(), calls=%async_computation.4 | async-start | bytes 16777216
  193.2 33.2 %copy-start.3 = (bf16[3456,8,64]{0,2,1:T(8,128)(2,1)S(1)}, bf16[3456,8,64]{0,2,1:T(8,128)(2,1)}, u32[]{:S(2)}) copy-start(bf16[3456,8,64]{0,2,1:T(8,128)(2,1)} %reshape.270) | copy-start | bytes 10616836
  272.2 5.3 copy-start.7
  273.1 6.6 copy-start.1
  279.7 2.8 copy-start.8
  282.5 0.7 copy-start.2
  294.4 5.3 copy-start.7
  295.3 6.6 copy-start.1
  301.9 2.8 copy-start.8
  304.7 0.7 copy-start.2
  316.6 5.3 copy-start.7
  317.4 6.6 copy-start.1
  324.0 2.8 copy-start.8
  326.8 0.7 copy-start.2
  338.8 5.3 copy-start.7
  339.6 6.6 copy-start.1
  346.3 2.8 copy-start.8
  349.1 0.7 copy-start.2
  365.9 6.6 copy-start.6
  365.9 6.6 copy-start.9
Sparse Core Ops, SparseCore 0:
  10.6 53.3 all-gather.10
  66.5 50.4 all-gather.12
  119.6 50.4 all-gather.16
  172.5 50.6 all-gather.14
  382.6 279.0 all-reduce.2
where the time goes:
time: 672 us; the launch traced here: 670 us
  waiting for transfers between devices  361 us (54%)
  matrix products  105 us (16%)
  local copies, waits for them, and re-layouts  88 us (13%)
  blocking collectives  76.3 us (11%)
  other arithmetic  25.2 us (4%)
  between operations  13.9 us (2%)
    unnamed x6, waiting for transfers between devices  273 us
    all_gather x1, waiting for transfers between devices, body(): lax.all_gather(key_rows, 'seq', axis=0, tiled=True)  48.2 us
    all_gather x1, waiting for transfers between devices, body(): lax.all_gather(value_rows, 'seq', axis=0, tiled=True)  39.4 us
    all_gather x1, blocking collectives, body(): lax.all_gather(row_max, 'seq', axis=0, tiled=True)  26 us
    all_gather x1, blocking collectives, body(): lax.all_gather(row_delta, 'seq', axis=0, tiled=True)  25.4 us
    all_gather x1, blocking collectives, body(): lax.all_gather(totals, 'seq', axis=0, tiled=True)  25 us
    dynamic_slice x32, local copies, waits for them, and re-layouts, body(): lax.scan(accumulate, (zero_sum, zero_sum), group_inputs)  24.2 us
    dot_general x4, matrix products, accumulate(): jnp.einsum('cqhd,ikhd->cihqk', group_query, own_keys, preferred_element_t...  21.5 us
  transfers between devices with their start and end apart: 5, of which 3 were waited for; matrix products, arithmetic and copies ran while one was open for 14% of the time, Pallas kernels for 0%

commit v1 on v0

--- a/solution.py
+++ b/solution.py
@@ -38,7 +38,9 @@
     )
     all_keys, all_values = (
         lax.all_gather(key_rows, "seq", axis=0, tiled=True),
-        lax.all_gather(value_rows, "seq", axis=0, tiled=True),
+        jnp.concatenate(
+            lax.all_to_all(jnp.stack([value_rows] * lax.axis_size("seq")), "seq", 0, 0), axis=0
+        ),
     )
     slab_blocks = all_keys.shape[0]
     first_block = lax.axis_index("seq") * local_blocks

time: 672 us -> 645 us (0.960)
  waiting for transfers between devices: 361 us -> 327 us
  starting transfers between devices: 0.21 us -> 8.13 us
    all_to_all x0 -> x1, waiting for transfers between devices: none -> 50.7 us  [body(): lax.all_to_all(jnp.stack([value_rows] * lax.axis_size('seq')), 'seq', 0, 0)]
    all_gather x1, waiting for transfers between devices: 48.2 us -> 2.85 us  [body(): lax.all_gather(key_rows, 'seq', axis=0, tiled=True)]
    all_gather x1 -> x0, waiting for transfers between devices: 39.4 us -> none  [body(): lax.all_gather(value_rows, 'seq', axis=0, tiled=True)]
    all_to_all x0 -> x1, starting transfers between devices: none -> 7.96 us  [body(): lax.all_to_all(jnp.stack([value_rows] * lax.axis_size('seq')), 'seq', 0, 0)]
    another operation x2 -> x3, local copies, waits for them, and re-layouts: 13.9 us -> 16.4 us
    unnamed x6 -> x5, waiting for transfers between devices: 273 us -> 274 us
where the time goes in v1:
time: 645 us; the launch traced here: 643 us
  waiting for transfers between devices  327 us (51%)
  matrix products  104 us (16%)
  local copies, waits for them, and re-layouts  87.8 us (14%)
  blocking collectives  75.5 us (12%)
  other arithmetic  25.2 us (4%)
  between operations  13.9 us (2%)
  starting transfers between devices  8.13 us (1%)
    unnamed x5, waiting for transfers between devices  274 us
    all_to_all x1, waiting for transfers between devices, body(): lax.all_to_all(jnp.stack([value_rows] * lax.axis_size('seq')), 'seq', 0, 0)  50.7 us
    all_gather x1, blocking collectives, body(): lax.all_gather(totals, 'seq', axis=0, tiled=True)  26 us
    all_gather x1, blocking collectives, body(): lax.all_gather(row_max, 'seq', axis=0, tiled=True)  25.2 us
    all_gather x1, blocking collectives, body(): lax.all_gather(row_delta, 'seq', axis=0, tiled=True)  24.3 us
    dynamic_slice x32, local copies, waits for them, and re-layouts, body(): lax.scan(accumulate, (zero_sum, zero_sum), group_inputs)  24.2 us
    dot_general x4, matrix products, accumulate(): jnp.einsum('cqhd,ikhd->cihqk', group_query, own_keys, preferred_element_t...  21.5 us
    dot_general x4, matrix products, accumulate(): jnp.einsum('cqhd,ikhd->cihqk', group_dattn, own_values, preferred_element...  17.8 us
  transfers between devices with their start and end apart: 5, of which 3 were waited for; matrix products, arithmetic and copies ran while one was open for 14% of the time, Pallas kernels for 0%

profile of v1, /device:TPU:97, one launch (start us, length us, event | category | flops | bytes accessed | tf_op | source)
XLA Modules:
  0.0 642.7 jit_solution(13522044247797428555)
XLA Ops:
  8.1 2.2 convolution_convert_fusion.2
  10.4 2.3 convolution_convert_fusion.1
  12.7 2.2 convolution_convert_fusion.3
  16.5 2.4 stack.3
  19.0 8.0 %all-to-all-start = ((bf16[32,1,128,512]{3,2,1,0:T(8,128)(2,1)}), bf16[32,1,128,512]{3,2,1,0:T(8,128)(2,1)}, u32[]{:S(2)}, u32[]{:S(2)}) async-start(bf16[32,1,128,512]{3,2,1,0:T(8,128)(2,1)} %stack.3), calls=%async_computation | async-start | bytes 8388608 | tf_op jit(solution)/shard_map/all_to_all | solution.py:42
  31.6 50.7 %all-to-all-done = bf16[32,1,128,512]{3,2,1,0:T(8,128)(2,1)} async-done(((bf16[32,1,128,512]{3,2,1,0:T(8,128)(2,1)}), bf16[32,1,128,512]{3,2,1,0:T(8,128)(2,1)}, u32[]{:S(2)}, u32[]{:S(2)}) %all-to-all-start) | async-done | bytes 4194336 | tf_op jit(solution)/shard_map/all_to_all | solution.py:42
  82.3 4.9 gather_fusion
  87.2 2.9 all-gather.9.cloned.1.call-done
  90.1 4.8 gather_fusion.1
  94.8 6.7 %bitcast_select_fusion.1 = (bf16[1,27,128,512]{3,2,1,0:T(8,128)(2,1)}, bf16[1,27,128,512]{3,2,1,0:T(8,128)(2,1)}) fusion(bf16[27,128,512]{2,1,0:T(8,128)(2,1)} %gather_fusion.1, pred[27]{0:T(512)(128)(4,1)S(1)} %and_bitcast_fusion, bf16[27,128,512]{2,1,0:T(8,128)(2,1)} %gather_fusion), kind=kLoop, calls=%fused_computation.42 | loop fusion | flops 3538944 | bytes 14155803 | tf_op jit(solution)/shard_map/jit(_take)/select_n | solution.py:52
  101.5 7.8 %copy.59 = bf16[1,27,128,512]{2,1,3,0:T(8,128)(2,1)} copy(bf16[1,27,128,512]{3,2,1,0:T(8,128)(2,1)} %get-tuple-element.173) | data formatting | bytes 7077888 | tf_op jit(solution)/shard_map/jit(_take)/select_n | solution.py:52
  109.3 7.0 %reshape.275 = bf16[3456,8,64]{0,2,1:T(8,128)(2,1)} reshape(bf16[1,27,128,512]{2,1,3,0:T(8,128)(2,1)} %copy.59) | data formatting | bytes 7077888 | tf_op jit(solution)/shard_map/reshape.49
  116.3 7.8 %copy.57 = bf16[1,27,128,512]{2,1,3,0:T(8,128)(2,1)} copy(bf16[1,27,128,512]{3,2,1,0:T(8,128)(2,1)} %get-tuple-element.174) | data formatting | bytes 7077888 | tf_op jit(solution)/shard_map/jit(_take)/select_n | solution.py:55
  124.1 7.0 %reshape.272 = bf16[3456,8,64]{0,2,1:T(8,128)(2,1)} reshape(bf16[1,27,128,512]{2,1,3,0:T(8,128)(2,1)} %copy.57) | data formatting | bytes 7077888 | tf_op jit(solution)/shard_map/reshape.52
  131.1 9.2 %fusion.27 = (f32[8,128]{1,0:T(8,128)S(1)}, f32[8,128,3456]{2,1,0:T(8,128)}) fusion(pred[3456]{0:T(1024)(128)(4,1)S(1)} %fusion.69, bf16[128,8,64]{0,2,1:T(8,128)(2,1)S(1)} %bitcast.236, bf16[3456,8,64]{0,2,1:T(8,128)(2,1)} %reshape.275), kind=kOutput, calls=%fused_computation.36 | convolution fusion | flops 463600640 | bytes 17833344 | tf_op jit(solution)/shard_map/bqhd,bkhd->bhqk/dot_general | solution.py:59
  140.3 25.2 %all-gather.2 = f32[256,128]{1,0:T(8,128)} all-gather(f32[8,128]{1,0:T(8,128)S(1)} %get-tuple-element.175), channel_id=4, replica_groups=mesh['seq'=32,'rep'=8] {'seq'}, dimensions={0}, use_global_device_ids=true | all-gather | bytes 135168 | tf_op jit(solution)/shard_map/all_gather | solution.py:110
  165.5 8.3 %fusion.28 = f32[8,128]{1,0:T(8,128)S(1)} fusion(f32[8,128,3456]{2,1,0:T(8,128)} %get-tuple-element.176, f32[8,128]{1,0:T(8,128)S(1)} %get-tuple-element.175, pred[3456]{0:T(1024)(128)(4,1)S(1)} %fusion.69), kind=kLoop, calls=%fused_computation.38 | loop fusion | flops 14154752 | bytes 14167424 | tf_op jit(solution)/shard_map/reduce_sum | solution.py:66
  173.7 26.0 %all-gather.3 = f32[256,128]{1,0:T(8,128)} all-gather(f32[8,128]{1,0:T(8,128)S(1)} %fusion.28), channel_id=5, replica_groups=mesh['seq'=32,'rep'=8] {'seq'}, dimensions={0}, use_global_device_ids=true | all-gather | bytes 135168 | tf_op jit(solution)/shard_map/all_gather | solution.py:111
  199.7 9.1 %multiply_reduce_fusion = (f32[128,8]{0,1:T(8,128)S(1)}, bf16[1,128,8,64]{1,3,2,0:T(8,128)(2,1)}) fusion(f32[1,128,8,64]{1,3,2,0:T(8,128)S(1)} %bitcast.246, f32[128,8]{0,1:T(8,128)S(1)} %bitcast.253, bf16[3456,8,64]{0,2,1:T(8,128)(2,1)S(1)} %copy-done.3, f32[8,128,3456]{2,1,0:T(8,128)} %get-tuple-element.176, f32[8,128]{1,0:T(8,128)S(1)} %get-tuple-element.175, ...), kind=kOutput, calls=%fused_computation.81 | convolution fusion | flops 467467264 | bytes 18103680 | tf_op jit(solution)/shard_map/bhqk,bkhd->bqhd/dot_general | solution.py:67
  208.8 24.3 %all_gather.23 = f32[32,8,128]{2,1,0:T(8,128)} all-gather(f32[1,8,128]{2,1,0:T(8,128)S(1)} %bitcast.254), channel_id=1, replica_groups=mesh['seq'=32,'rep'=8] {'seq'}, dimensions={0}, use_global_device_ids=true | all-gather | bytes 135168 | tf_op jit(solution)/shard_map/all_gather | solution.py:112
  233.1 88.9 %while.13 = (s32[]{:T(128)}, f32[1,128,8,64]{1,3,2,0:T(8,128)}, f32[1,128,8,64]{1,3,2,0:T(8,128)}, bf16[4,8,128,512]{3,2,1,0:T(8,128)(2,1)}, pred[4,8,1]{1,2,0:T...) while((s32[]{:T(128)}, f32[1,128,8,64]{1,3,2,0:T(8,128)}, ...), condition=%wide.region_5.7_spmd.clone, body=%wide.region_4.6_spmd.clone.sunk | while | flops 545521664 | bytes 35356956 | solution.py:167
  233.1 1.7 constant_dynamic-slice_fusion.10
  238.4 5.4 fusion.112
  245.3 4.4 fusion.113
  249.7 2.2 fusion.114
  251.9 2.8 fusion.115
  255.4 1.7 constant_dynamic-slice_fusion.10
  260.6 5.4 fusion.112
  267.5 4.4 fusion.113
  271.9 2.2 fusion.114
  274.1 2.8 fusion.115
  282.8 5.4 fusion.112
  289.7 4.4 fusion.113
  294.1 2.2 fusion.114
  296.3 2.8 fusion.115
  305.0 5.4 fusion.112
  311.9 4.4 fusion.113
  316.3 2.2 fusion.114
  318.5 2.8 fusion.115
  323.9 10.6 %fusion.51 = bf16[8,64,128]{2,1,0:T(8,128)(2,1)S(1)} fusion(bf16[3456,8,64]{0,2,1:T(8,128)(2,1)} %reshape.275, bf16[128,8,64]{0,2,1:T(8,128)(2,1)} %bitcast.251, bf16[3456,8,64]{0,2,1:T(8,128)(2,1)} %reshape.272, f32[8,128,3456]{2,1,0:T(8,128)} %get-tuple-element.176, f32[8,128]{1,0:T(8,128)S(1)} %bitcast.255, f32[8,128]{1,0:T(8,128)S(1)} %fusion.28, ...), kind=kOutput, calls=%fused_computation.62 | convolution fusion | flops 930873344 | bytes 21511552 | tf_op jit(solution)/shard_map/bhqk,bkhd->bqhd/dot_general | solution.py:99
  334.5 3.6 fusion.64
  338.1 6.6 %copy.70 = f32[1024,3,512]{2,0,1:T(8,128)} copy(f32[1024,3,512]{0,2,1:T(8,128)} %bitcast.227) | data formatting | bytes 12582912 | tf_op jit(solution)/shard_map/reshape | solution.py:181
  345.2 1.8 copy.71
  347.0 7.6 %pad_maximum_fusion = f32[4,1024,512]{2,1,0:T(8,128)} fusion(f32[1,1024,512]{2,1,0:T(8,128)} %copy.71, f32[3,1024,512]{2,1,0:T(8,128)} %bitcast.230), kind=kLoop, calls=%fused_computation.37 | loop fusion | flops 2097152 | bytes 16777216 | tf_op jit(solution)/shard_map/concatenate | solution.py:182
  354.7 2.1 slice_bitcast_fusion.1
  356.7 2.4 fusion.43
  359.1 1.9 fusion.44
  361.0 273.6 %all-reduce.3.cloned.1.call-done = f32[4,1024,512]{2,1,0:T(8,128)} async-done(((f32[4,1024,512]{2,1,0:T(8,128)}), f32[4,1024,512]{2,1,0:T(8,128)}) %all-reduce.3.cloned.1.call-update) | async-done | bytes 8388624
  (115 shorter events, 37.0 us)
Async XLA Ops:
  7.2 1.0 copy-start
  7.2 82.9 %all-gather.9.cloned.1.call-start = ((), (), s32[]{:S(2)}) async-start(), calls=%async_computation.1 | async-start | bytes 4325376 | tf_op jit(solution)/shard_map/all_gather | solution.py:40
  10.3 222.8 %all-gather.13.cloned.1.call-start = ((), (), s32[]{:S(2)}) async-start(), calls=%async_computation.3 | async-start | bytes 4325376 | tf_op jit(solution)/shard_map/all_gather | solution.py:107
  12.7 220.4 %all-gather.11.cloned.1.call-start = ((), (), s32[]{:S(2)}) async-start(), calls=%async_computation.2 | async-start | bytes 4325376 | tf_op jit(solution)/shard_map/all_gather | solution.py:106
  19.0 8.0 %copy-start.5 = (bf16[128,512]{1,0:T(8,128)(2,1)S(1)}, bf16[128,512]{1,0:T(8,128)(2,1)}, u32[]{:S(2)}) copy-start(bf16[128,512]{1,0:T(8,128)(2,1)} %convolution_convert_fusion.3) | copy-start | bytes 393220
  19.0 8.2 %copy-start.4 = (bf16[128,512]{1,0:T(8,128)(2,1)S(1)}, bf16[128,512]{1,0:T(8,128)(2,1)}, u32[]{:S(2)}) copy-start(bf16[128,512]{1,0:T(8,128)(2,1)} %convolution_convert_fusion.1) | copy-start | bytes 393220
  19.0 9.1 %copy-start.6 = (bf16[128,512]{1,0:T(8,128)(2,1)S(1)}, bf16[128,512]{1,0:T(8,128)(2,1)}, u32[]{:S(2)}) copy-start(bf16[128,512]{1,0:T(8,128)(2,1)} %convolution_convert_fusion.2) | copy-start | bytes 393220
  19.0 10.0 %copy-start.12 = (s32[1,32]{1,0:T(1,128)S(1)}, s32[1,32]{1,0:T(1,128)}, u32[]{:S(2)}) copy-start(s32[1,32]{1,0:T(1,128)} %param.13) | copy-start | bytes 388
  19.0 10.5 %copy-start.11 = (s32[1,32,27]{1,0,2:T(1,128)S(1)}, s32[1,32,27]{1,0,2:T(1,128)}, u32[]{:S(2)}) copy-start(s32[1,32,27]{1,0,2:T(1,128)} %param.12) | copy-start | bytes 10372
  19.0 63.3 %all-to-all-start = ((bf16[32,1,128,512]{3,2,1,0:T(8,128)(2,1)}), bf16[32,1,128,512]{3,2,1,0:T(8,128)(2,1)}, u32[]{:S(2)}, u32[]{:S(2)}) async-start(bf16[32,1,128,512]{3,2,1,0:T(8,128)(2,1)} %stack.3), calls=%async_computation | async-start | bytes 8388608 | tf_op jit(solution)/shard_map/all_to_all | solution.py:42
  26.9 607.7 %all-reduce.3.cloned.1.call-start = ((), (), s32[]{:S(2)}) async-start(), calls=%async_computation.4 | async-start | bytes 16777216
  165.4 34.3 %copy-start.3 = (bf16[3456,8,64]{0,2,1:T(8,128)(2,1)S(1)}, bf16[3456,8,64]{0,2,1:T(8,128)(2,1)}, u32[]{:S(2)}) copy-start(bf16[3456,8,64]{0,2,1:T(8,128)(2,1)} %reshape.272) | copy-start | bytes 10616836
  244.5 5.3 copy-start.8
  245.3 6.6 %copy-start.1 = (f32[1,128,8,64]{1,3,2,0:T(8,128)S(1)}, f32[1,128,8,64]{1,3,2,0:T(8,128)}, u32[]{:S(2)}) copy-start(f32[1,128,8,64]{1,3,2,0:T(8,128)} %get-tuple-element.269) | copy-start | bytes 786436 | tf_op jit(solution)/shard_map/while
  251.9 2.8 copy-start.9
  254.7 0.7 copy-start.2
  266.7 5.3 copy-start.8
  267.5 6.6 %copy-start.1 = (f32[1,128,8,64]{1,3,2,0:T(8,128)S(1)}, f32[1,128,8,64]{1,3,2,0:T(8,128)}, u32[]{:S(2)}) copy-start(f32[1,128,8,64]{1,3,2,0:T(8,128)} %get-tuple-element.269) | copy-start | bytes 786436 | tf_op jit(solution)/shard_map/while
  274.1 2.8 copy-start.9
  276.9 0.7 copy-start.2
  288.8 5.3 copy-start.8
  289.6 6.6 %copy-start.1 = (f32[1,128,8,64]{1,3,2,0:T(8,128)S(1)}, f32[1,128,8,64]{1,3,2,0:T(8,128)}, u32[]{:S(2)}) copy-start(f32[1,128,8,64]{1,3,2,0:T(8,128)} %get-tuple-element.269) | copy-start | bytes 786436 | tf_op jit(solution)/shard_map/while
  296.3 2.8 copy-start.9
  299.1 0.7 copy-start.2
  311.1 5.3 copy-start.8
  311.9 6.6 %copy-start.1 = (f32[1,128,8,64]{1,3,2,0:T(8,128)S(1)}, f32[1,128,8,64]{1,3,2,0:T(8,128)}, u32[]{:S(2)}) copy-start(f32[1,128,8,64]{1,3,2,0:T(8,128)} %get-tuple-element.269) | copy-start | bytes 786436 | tf_op jit(solution)/shard_map/while
  318.5 2.8 copy-start.9
  321.3 0.7 copy-start.2
  338.1 6.6 %copy-start.7 = (bf16[1,128,1024]{2,1,0:T(8,128)(2,1)S(1)}, bf16[1,128,1024]{2,1,0:T(8,128)(2,1)}, u32[]{:S(2)}) copy-start(bf16[1,128,1024]{2,1,0:T(8,128)(2,1)} %param.10) | copy-start | bytes 786436
  338.1 6.6 %copy-start.10 = (bf16[1,128,8,64]{1,3,2,0:T(8,128)(2,1)S(1)}, bf16[1,128,8,64]{1,3,2,0:T(8,128)(2,1)}, u32[]{:S(2)}) copy-start(bf16[1,128,8,64]{1,3,2,0:T(8,128)(2,1)} %get-tuple-element.178) | copy-start | bytes 393220
Sparse Core Ops, SparseCore 0:
  10.5 79.4 all-gather.8
  92.6 50.7 all-gather.12
  146.0 50.8 all-gather.10
  354.8 279.8 all-reduce.2
